TPU v7x, 32 devices: a whole 2x2x4 slice. The times are simulated.
32 devices in a mesh: band: 4 (over y, core), space: 8 (over z, x).
Axes of the slice: x: 2, y: 2, z: 4, core: 2. Of those that a mesh axis runs over, the one named last changes fastest.
Arguments:
- states: float32 [256, 48, 1024], P('band', 'space'), may hold values from -6 to 6
- patch_ids: int32 [48, 32], P('space'), may hold values from 0 to 63
- metric_table: float32 [64, 96], replicated, may hold values from 0.5 to 2
- potential: float32 [48, 1024], P('space'), may hold values from -3 to 0
Outputs:
- orthonormal: float32 [256, 48, 1024], P(None, 'space', 'band')
All inputs are finite; a program needn't handle non-finite values.
Results may differ from a plain program's by a relative error of at most 0.00014.
Values sent between devices are 32-bit elements; how exact they have to be, the bound alone decides.
A program may use at most 64 MiB of HBM per device.

v0:
```python
import jax
import jax.numpy as jnp
from jax import lax
from jax.sharding import PartitionSpec as P

DEGREE = 3
NY = 32
NZ = 32
CENTRE = 8.5
HALF_WIDTH = 7.5
OFFSETS = (-2, -1, 0, 1, 2)
WEIGHTS = (-1.0 / 12.0, 4.0 / 3.0, -2.5, 4.0 / 3.0, -1.0 / 12.0)


def with_halo(cells, sides, width):
    for axis, dim in sides:
        count = lax.axis_size(axis)
        ends = count - 1
        head = lax.slice_in_dim(cells, 0, width, axis=dim)
        tail = lax.slice_in_dim(cells, cells.shape[dim] - width, cells.shape[dim], axis=dim)
        cells = jnp.concatenate(
            [
                lax.ppermute(tail, axis, [(i, (i + 1) % count) for i in range(ends)]),
                cells,
                lax.ppermute(head, axis, [((i + 1) % count, i) for i in range(ends)]),
            ],
            axis=dim,
        )
    return cells


def swapped(value, axis, bit):
    mask = 2**bit
    pairs = [(source, source ^ mask) for source in range(lax.axis_size(axis))]
    return lax.ppermute(value, axis, pairs)


def apply_ham(extended, potential, metric, z_weights):
    planes = extended.shape[1] - 4
    plane_cells = extended.shape[2]
    block = extended[:, 2 : 2 + planes, :]
    row_pad = 2 * NZ
    padded = jnp.pad(block, ((0, 0), (0, 0), (row_pad, row_pad)))
    x_term = WEIGHTS[0] * extended[:, 2 + OFFSETS[0] : 2 + OFFSETS[0] + planes, :]
    y_term = (
        WEIGHTS[0]
        * padded[:, :, row_pad + OFFSETS[0] * NZ : row_pad + OFFSETS[0] * NZ + plane_cells]
    )
    z_term = z_weights[0] * padded[:, :, row_pad + OFFSETS[0] : row_pad + OFFSETS[0] + plane_cells]
    for position in range(1, 5):
        offset = OFFSETS[position]
        weight = WEIGHTS[position]
        x_term = x_term + weight * extended[:, 2 + offset : 2 + offset + planes, :]
        y_term = (
            y_term
            + weight * padded[:, :, row_pad + offset * NZ : row_pad + offset * NZ + plane_cells]
        )
        z_term = (
            z_term
            + z_weights[position] * padded[:, :, row_pad + offset : row_pad + offset + plane_cells]
        )
    kinetic = metric[0] * x_term + metric[1] * y_term + metric[2] * z_term
    return potential * block - 0.5 * kinetic


def on_device(states, patch_ids, metric_table, potential):
    planes = states.shape[1]
    plane_cells = states.shape[2]
    one_hot = (patch_ids[:, :, None] == jnp.arange(metric_table.shape[0], dtype=jnp.int32)).astype(
        jnp.float32
    )
    looked = jnp.einsum("xyp,pm->xym", one_hot, metric_table, precision=lax.Precision.HIGHEST)
    metric = looked.reshape(planes, NY, 3, NZ).transpose(2, 0, 1, 3).reshape(3, planes, plane_cells)
    z_index = jnp.arange(plane_cells, dtype=jnp.int32) % NZ
    z_weights = [
        WEIGHTS[position]
        * ((z_index + OFFSETS[position] >= 0) & (z_index + OFFSETS[position] < NZ)).astype(
            jnp.float32
        )
        for position in range(5)
    ]

    def step_ham(block):
        extended = with_halo(block, (("space", 1),), 2)
        return apply_ham(extended, potential, metric, z_weights)

    applied = step_ham(states)
    earlier = states
    current = (applied - CENTRE * states) / HALF_WIDTH
    for degree_step in range(DEGREE - 1):
        applied = step_ham(current)
        following = 2.0 * (applied - CENTRE * current) / HALF_WIDTH - earlier
        earlier = current
        current = following
    regrouped = lax.all_to_all(current, "band", split_axis=2, concat_axis=0, tiled=True)
    all_states = regrouped.shape[0]
    flat = regrouped.reshape(all_states, -1)
    cell_total = planes * plane_cells * lax.axis_size("space")
    local_gram = jnp.dot(
        flat, flat.T, precision=lax.Precision.HIGHEST, preferred_element_type=jnp.float32
    )
    device_index = lax.axis_index(("band", "space"))
    levels = lax.axis_size(("band", "space")).bit_length() - 1
    vector = local_gram.reshape(-1)
    for level in range(levels):
        bit = levels - 1 - level
        half = vector.shape[0] // 2
        upper_side = device_index >> bit & 1 == 1
        kept = jnp.where(upper_side, vector[half:], vector[:half])
        sending = jnp.where(upper_side, vector[:half], vector[half:])
        vector = kept + swapped(sending, ("band", "space"), bit)
    for level in range(levels):
        bit = level
        upper_side = device_index >> bit & 1 == 1
        received = swapped(vector, ("band", "space"), bit)
        vector = jnp.where(
            upper_side, jnp.concatenate([received, vector]), jnp.concatenate([vector, received])
        )
    gram = vector.reshape(all_states, all_states) / cell_total
    factor = jnp.linalg.cholesky(gram)
    result = lax.linalg.triangular_solve(factor, flat, left_side=True, lower=True)
    return result.reshape(all_states, planes, regrouped.shape[2])


def solution(mesh):
    return jax.shard_map(
        on_device,
        mesh=mesh,
        in_specs=(P("band", "space", None), P("space", None), P(), P("space", None)),
        out_specs=P(None, "space", "band"),
        check_vma=False,
    )
```

profile of v0, /device:TPU:0, one launch (start us, length us, event | category | flops | bytes accessed | tf_op | source)
XLA Modules:
  0.0 248.5 jit_solution(1068636462713036321)
XLA Ops:
  0.0 2.3 fusion.143
  2.3 5.0 %collective-permute-start = (f32[64,2,1024]{2,0,1:T(8,128)}, f32[64,2,1024]{2,0,1:T(8,128)S(1)}, u32[]{:S(2)}, u32[]{:S(2)}) collective-permute-start(f32[64,2,1024]{2,0,1:T(8,128)} %get-tuple-element.36), channel_id=1, source_target_pairs={{0,1},{1,2},{2,3},{3,4},{4,5},{5,6},{6,7},{8,9},{9,10},{10,11},{11... | collective-permute-start | bytes 1572872 | tf_op jit(solution)/shard_map/ppermute | solution.py:23
  7.3 1.3 collective-permute-start.1
  8.6 0.2 fusion.102
  8.9 0.2 reshape.103
  9.1 0.8 slice_reduce_fusion.2
  10.3 19.7 %collective-permute-done = f32[64,2,1024]{2,0,1:T(8,128)S(1)} collective-permute-done((f32[64,2,1024]{2,0,1:T(8,128)}, f32[64,2,1024]{2,0,1:T(8,128)S(1)}, u32[]{:S(2)}, u32[]{:S(2)}) %collective-permute-start) | collective-permute-done | bytes 524320 | tf_op jit(solution)/shard_map/ppermute | solution.py:23
  30.1 0.2 constant_dynamic-update-slice_fusion
  30.4 0.5 copy-done.2
  30.8 3.6 %broadcast_multiply_fusion = (f32[64,6,1024]{2,0,1:T(8,128)S(1)}, f32[64,6,1024]{2,0,1:T(8,128)S(1)}) fusion(f32[64,6,1024]{2,0,1:T(8,128)S(1)} %copy-done.1, f32[1024]{0:T(1024)S(1)} %get-tuple-element.48, f32[1024]{0:T(1024)S(1)} %get-tuple-element.49, f32[1024]{0:T(1024)S(1)} %fusion.136, f32[1024]{0:T(1024)S(1)} %get-tuple-element.50, ...), kind=kLoop, calls=%fused_computation.145 | loop fusion | flops 14548992 | bytes 11128832 | tf_op jit(solution)/shard_map/div | solution.py:89
  34.5 4.3 %collective-permute-start.2 = (f32[64,2,1024]{2,0,1:T(8,128)S(1)}, f32[64,2,1024]{2,0,1:T(8,128)S(1)}, u32[]{:S(2)}, u32[]{:S(2)}) collective-permute-start(f32[64,2,1024]{2,0,1:T(8,128)S(1)} %get-tuple-element.32), channel_id=1, source_target_pairs={{0,1},{1,2},{2,3},{3,4},{4,5},{5,6},{6,7},{8,9},{9,10},{10,11},{11... | collective-permute-start | bytes 1572872 | tf_op jit(solution)/shard_map/ppermute | solution.py:23
  38.8 1.3 collective-permute-start.3
  40.1 20.2 %collective-permute-done.2 = f32[64,2,1024]{2,0,1:T(8,128)S(1)} collective-permute-done((f32[64,2,1024]{2,0,1:T(8,128)S(1)}, f32[64,2,1024]{2,0,1:T(8,128)S(1)}, u32[]{:S(2)}, u32[]{:S(2)}) %collective-permute-start.2) | collective-permute-done | bytes 524320 | tf_op jit(solution)/shard_map/ppermute | solution.py:23
  60.3 3.8 %fusion.35 = f32[64,6,1024]{2,0,1:T(8,128)S(1)} fusion(f32[64,6,1024]{2,0,1:T(8,128)S(1)} %copy-done.1, f32[64,6,1024]{2,0,1:T(8,128)S(1)} %get-tuple-element.24, f32[64,2,1024]{2,0,1:T(8,128)S(1)} %collective-permute-done.3, f32[64,2,1024]{2,0,1:T(8,128)S(1)} %collective-permute-done.2, f32[64,6,1024]{2,0,1:T(8,128)S(1)} %get-tuple-element.25, ...), kind=kLoop, calls=%fused_computation.70 | loop fusion | flops 16515072 | bytes 7458816 | tf_op jit(solution)/shard_map/sub | solution.py:92
  64.3 4.4 %collective-permute-start.4 = (f32[64,2,1024]{2,0,1:T(8,128)S(1)}, f32[64,2,1024]{2,0,1:T(8,128)S(1)}, u32[]{:S(2)}, u32[]{:S(2)}) collective-permute-start(f32[64,2,1024]{2,0,1:T(8,128)S(1)} %get-tuple-element.30), channel_id=1, source_target_pairs={{0,1},{1,2},{2,3},{3,4},{4,5},{5,6},{6,7},{8,9},{9,10},{10,11},{11... | collective-permute-start | bytes 1572872 | tf_op jit(solution)/shard_map/ppermute | solution.py:23
  68.7 1.3 collective-permute-start.5
  70.0 19.4 %collective-permute-done.4 = f32[64,2,1024]{2,0,1:T(8,128)S(1)} collective-permute-done((f32[64,2,1024]{2,0,1:T(8,128)S(1)}, f32[64,2,1024]{2,0,1:T(8,128)S(1)}, u32[]{:S(2)}, u32[]{:S(2)}) %collective-permute-start.4) | collective-permute-done | bytes 524320 | tf_op jit(solution)/shard_map/ppermute | solution.py:23
  89.3 3.8 %fusion.60 = f32[64,6,1024]{2,0,1:T(8,128)S(1)} fusion(f32[64,6,1024]{2,0,1:T(8,128)S(1)} %fusion.35, f32[64,2,1024]{2,0,1:T(8,128)S(1)} %collective-permute-done.5, f32[64,2,1024]{2,0,1:T(8,128)S(1)} %collective-permute-done.4, f32[64,6,1024]{2,0,1:T(8,128)S(1)} %get-tuple-element.25, f32[1024]{0:T(1024)S(1)} %get-tuple-element.48, ...), kind=kLoop, calls=%fused_computation.95 | loop fusion | flops 16908288 | bytes 5885952 | tf_op jit(solution)/shard_map/sub | solution.py:92
  93.1 2.7 %copy.48 = f32[64,6,1024]{0,1,2:T(8,128)} copy(f32[64,6,1024]{2,0,1:T(8,128)S(1)} %fusion.60) | data formatting | bytes 3145728 | tf_op jit(solution)/shard_map/sub | solution.py:92
  95.9 5.1 %reshape.143 = f32[4,1,98304]{2,1,0:T(1,128)} reshape(f32[1024,6,64]{2,1,0:T(8,128)} %bitcast.60) | data formatting | bytes 3145728
  101.0 3.7 %all-to-all-start = ((f32[4,1,98304]{2,1,0:T(1,128)}), f32[4,1,98304]{2,1,0:T(1,128)S(1)}, u32[]{:S(2)}, u32[]{:S(2)}) async-start(f32[4,1,98304]{2,1,0:T(1,128)} %reshape.143), calls=%async_computation | async-start | bytes 3145728 | tf_op jit(solution)/shard_map/all_to_all | solution.py:95
  104.7 19.8 %all-to-all-done = f32[4,1,98304]{2,1,0:T(1,128)S(1)} async-done(((f32[4,1,98304]{2,1,0:T(1,128)}), f32[4,1,98304]{2,1,0:T(1,128)S(1)}, u32[]{:S(2)}, u32[]{:S(2)}) %all-to-all-start) | async-done | bytes 1572896 | tf_op jit(solution)/shard_map/all_to_all | solution.py:95
  124.6 0.5 broadcast.404
  125.1 5.2 %reduce.24 = f32[4,98304]{1,0:T(4,128)S(1)} reduce(f32[4,1,98304]{2,1,0:T(1,128)S(1)} %all-to-all-done, f32[]{:T(128)} %broadcast.404), dimensions={1}, to_apply=%all_to_all.11.reduce_sub_computation | reduce | bytes 3145732 | tf_op jit(solution)/shard_map/all_to_all | solution.py:95
  130.3 3.6 %reshape.144 = f32[1024,6,64]{2,1,0:T(8,128)} reshape(f32[4,98304]{1,0:T(4,128)S(1)} %reduce.24) | data formatting | bytes 3145728
  133.9 3.3 %copy.49 = f32[64,6,4,256]{3,1,0,2:T(8,128)S(1)} copy(f32[64,6,4,256]{0,1,3,2:T(8,128)} %bitcast.61) | data formatting | bytes 3145728 | tf_op jit(solution)/shard_map/all_to_all | solution.py:95
  137.2 0.7 copy.61
  137.9 1.4 fusion.144
  139.4 0.5 collective-permute-start.6
  140.0 4.5 %collective-permute-done.6 = f32[32768]{0:T(1024)S(1)} collective-permute-done((f32[32768]{0:T(1024)S(1)}, f32[32768]{0:T(1024)S(1)}, u32[]{:S(2)}, u32[]{:S(2)}) %collective-permute-start.6) | collective-permute-done | bytes 131104 | tf_op jit(solution)/shard_map/ppermute | solution.py:35
  144.6 1.2 collective-permute-done.7
  145.8 8.5 %collective-permute-start.8 = (f32[8192]{0:T(1024)S(1)}, f32[8192]{0:T(1024)S(1)}, u32[]{:S(2)}, u32[]{:S(2)}) collective-permute-start(f32[8192]{0:T(1024)S(1)} %slice_select_fusion.1), channel_id=1, source_target_pairs={{0,4},{1,5},{2,6},{3,7},{4,0},{5,1},{6,2},{7,3},{8,12},{9,13},{10,... | collective-permute-start | bytes 98312 | tf_op jit(solution)/shard_map/ppermute | solution.py:35
  154.4 1.9 collective-permute-done.8
  156.3 2.0 collective-permute-start.9
  158.3 1.8 collective-permute-done.9
  160.2 3.6 %collective-permute-done.10 = f32[2048]{0:T(1024)S(1)} collective-permute-done((f32[2048]{0:T(1024)S(1)}, f32[2048]{0:T(1024)S(1)}, u32[]{:S(2)}, u32[]{:S(2)}) %collective-permute-start.10) | collective-permute-done | bytes 8224 | tf_op jit(solution)/shard_map/ppermute | solution.py:35
  163.9 3.6 %collective-permute-done.11 = f32[2048]{0:T(1024)S(1)} collective-permute-done((f32[2048]{0:T(1024)S(1)}, f32[2048]{0:T(1024)S(1)}, u32[]{:S(2)}, u32[]{:S(2)}) %collective-permute-start.11) | collective-permute-done | bytes 8224 | tf_op jit(solution)/shard_map/ppermute | solution.py:35
  167.5 1.9 collective-permute-start.12
  169.5 0.3 copy.64
  169.8 0.3 copy.65
  170.1 1.1 collective-permute-done.12
  171.2 2.9 %collective-permute-start.13 = (f32[8192]{0:T(1024)S(1)}, f32[8192]{0:T(1024)S(1)}, u32[]{:S(2)}, u32[]{:S(2)}) collective-permute-start(f32[8192]{0:T(1024)S(1)} %maximum_select_fusion.5), channel_id=1, source_target_pairs={{0,4},{1,5},{2,6},{3,7},{4,0},{5,1},{6,2},{7,3},{8,12},{9,13},{10,... | collective-permute-start | bytes 98312 | tf_op jit(solution)/shard_map/ppermute | solution.py:35
  174.4 1.7 collective-permute-done.13
  176.3 1.1 collective-permute-done.14
  177.4 0.6 collective-permute-start.15
  178.4 4.6 %collective-permute-done.15 = f32[32768]{0:T(1024)S(1)} collective-permute-done((f32[32768]{0:T(1024)S(1)}, f32[32768]{0:T(1024)S(1)}, u32[]{:S(2)}, u32[]{:S(2)}) %collective-permute-start.15) | collective-permute-done | bytes 131104 | tf_op jit(solution)/shard_map/ppermute | solution.py:35
  183.4 11.7 %cholesky.50 = f32[128,128]{1,0:T(8,128)S(1)} custom-call(f32[128,128]{1,0:T(8,128)S(1)} %cholesky.118), custom_call_target="Cholesky" | custom-call | tf_op jit(solution)/shard_map/jit(cholesky)/cholesky | solution.py:120
  195.2 9.8 %custom-call.14 = f32[1,128,128]{1,2,0:T(8,128)S(1)} custom-call(f32[1,128,128]{2,1,0:T(8,128)S(1)} %get-tuple-element.43), custom_call_target="InvertDiagBlocksLowerTriangular" | custom-call | tf_op jit(solution)/shard_map/jit(cholesky)/cholesky | solution.py:120
  205.0 0.2 constant_dynamic-update-slice_fusion.5
  205.2 0.3 convolution_subtract_fusion.1
  205.5 12.0 %cholesky.105 = f32[128,128]{1,0:T(8,128)S(1)} custom-call(f32[128,128]{1,0:T(8,128)S(1)} %convolution_subtract_fusion.1), custom_call_target="Cholesky" | custom-call | tf_op jit(solution)/shard_map/jit(cholesky)/cholesky | solution.py:120
  217.4 0.7 compare_reduce_fusion
  218.2 0.7 compare_reduce_fusion.1
  220.2 4.0 %while.1 = (s32[]{:T(128)}, f32[256,256]{1,0:T(8,128)S(1)}, s32[2,2]{1,0:T(2,128)S(1)}, f32[2,128,128]{2,1,0:T(8,128)S(1)}, s32[]{:T(128)}) while((s32[]{:T(128)}, f32[256,256]{1,0:T(8,128)S(1)}, s32[2,2]{1,0:T(2,128)S(1)}, f32[2,128,128]{2,1,0:T(8,128)S(1)}, s32[]{:T(128)}) %tuple.34), condition=%wide.while_cond, body=%wide.while_body.sunk | while | flops 2 | bytes 131181 | solution.py:121
  220.2 0.6 fusion.153
  220.8 1.3 bitcast_dynamic-update-slice_fusion.2
  222.2 0.6 fusion.153
  222.8 1.3 bitcast_dynamic-update-slice_fusion.2
  224.2 19.7 %custom-call.15 = f32[2,128,128]{1,2,0:T(8,128)S(1)} custom-call(f32[2,128,128]{2,1,0:T(8,128)S(1)} %get-tuple-element.12), custom_call_target="InvertDiagBlocksLowerTriangular" | custom-call | tf_op jit(solution)/shard_map/triangular_solve | solution.py:121
  243.8 0.8 fusion.105
  244.7 0.8 convolution_subtract_fusion
  245.5 0.8 fusion.104
  246.4 0.5 copy.59
  246.9 1.6 copy.60
  (71 shorter events, 2.6 us)
Async XLA Ops:
  0.0 8.6 %copy-start = (f32[64,96]{1,0:T(8,128)S(1)}, f32[64,96]{1,0:T(8,128)}, u32[]{:S(2)}) copy-start(f32[64,96]{1,0:T(8,128)} %param.6) | copy-start | bytes 73732
  0.0 8.6 %copy-start.3 = (s32[6,32]{1,0:T(8,128)S(1)}, s32[6,32]{1,0:T(8,128)}, u32[]{:S(2)}) copy-start(s32[6,32]{1,0:T(8,128)} %param.5) | copy-start | bytes 2308
  2.3 27.8 %copy-start.1 = (f32[64,6,1024]{2,0,1:T(8,128)S(1)}, f32[64,6,1024]{2,0,1:T(8,128)}, u32[]{:S(2)}) copy-start(f32[64,6,1024]{2,0,1:T(8,128)} %param.4) | copy-start | bytes 4718596
  2.3 27.7 %collective-permute-start = (f32[64,2,1024]{2,0,1:T(8,128)}, f32[64,2,1024]{2,0,1:T(8,128)S(1)}, u32[]{:S(2)}, u32[]{:S(2)}) collective-permute-start(f32[64,2,1024]{2,0,1:T(8,128)} %get-tuple-element.36), channel_id=1, source_target_pairs={{0,1},{1,2},{2,3},{3,4},{4,5},{5,6},{6,7},{8,9},{9,10},{10,11},{11... | collective-permute-start | bytes 1572872 | tf_op jit(solution)/shard_map/ppermute | solution.py:23
  7.3 23.0 %collective-permute-start.1 = (f32[64,2,1024]{2,0,1:T(8,128)}, f32[64,2,1024]{2,0,1:T(8,128)S(1)}, u32[]{:S(2)}, u32[]{:S(2)}) collective-permute-start(f32[64,2,1024]{2,0,1:T(8,128)} %get-tuple-element.37), channel_id=1, source_target_pairs={{1,0},{2,1},{3,2},{4,3},{5,4},{6,5},{7,6},{9,8},{10,9},{11,10},{12... | collective-permute-start | bytes 1572872 | tf_op jit(solution)/shard_map/ppermute | solution.py:25
  30.1 0.8 copy-start.2
  34.5 25.8 %collective-permute-start.2 = (f32[64,2,1024]{2,0,1:T(8,128)S(1)}, f32[64,2,1024]{2,0,1:T(8,128)S(1)}, u32[]{:S(2)}, u32[]{:S(2)}) collective-permute-start(f32[64,2,1024]{2,0,1:T(8,128)S(1)} %get-tuple-element.32), channel_id=1, source_target_pairs={{0,1},{1,2},{2,3},{3,4},{4,5},{5,6},{6,7},{8,9},{9,10},{10,11},{11... | collective-permute-start | bytes 1572872 | tf_op jit(solution)/shard_map/ppermute | solution.py:23
  38.8 21.5 %collective-permute-start.3 = (f32[64,2,1024]{2,0,1:T(8,128)S(1)}, f32[64,2,1024]{2,0,1:T(8,128)S(1)}, u32[]{:S(2)}, u32[]{:S(2)}) collective-permute-start(f32[64,2,1024]{2,0,1:T(8,128)S(1)} %get-tuple-element.33), channel_id=1, source_target_pairs={{1,0},{2,1},{3,2},{4,3},{5,4},{6,5},{7,6},{9,8},{10,9},{11,10},{12... | collective-permute-start | bytes 1572872 | tf_op jit(solution)/shard_map/ppermute | solution.py:25
  64.3 25.1 %collective-permute-start.4 = (f32[64,2,1024]{2,0,1:T(8,128)S(1)}, f32[64,2,1024]{2,0,1:T(8,128)S(1)}, u32[]{:S(2)}, u32[]{:S(2)}) collective-permute-start(f32[64,2,1024]{2,0,1:T(8,128)S(1)} %get-tuple-element.30), channel_id=1, source_target_pairs={{0,1},{1,2},{2,3},{3,4},{4,5},{5,6},{6,7},{8,9},{9,10},{10,11},{11... | collective-permute-start | bytes 1572872 | tf_op jit(solution)/shard_map/ppermute | solution.py:23
  68.7 20.7 %collective-permute-start.5 = (f32[64,2,1024]{2,0,1:T(8,128)S(1)}, f32[64,2,1024]{2,0,1:T(8,128)S(1)}, u32[]{:S(2)}, u32[]{:S(2)}) collective-permute-start(f32[64,2,1024]{2,0,1:T(8,128)S(1)} %get-tuple-element.31), channel_id=1, source_target_pairs={{1,0},{2,1},{3,2},{4,3},{5,4},{6,5},{7,6},{9,8},{10,9},{11,10},{12... | collective-permute-start | bytes 1572872 | tf_op jit(solution)/shard_map/ppermute | solution.py:25
  101.0 23.6 %all-to-all-start = ((f32[4,1,98304]{2,1,0:T(1,128)}), f32[4,1,98304]{2,1,0:T(1,128)S(1)}, u32[]{:S(2)}, u32[]{:S(2)}) async-start(f32[4,1,98304]{2,1,0:T(1,128)} %reshape.143), calls=%async_computation | async-start | bytes 3145728 | tf_op jit(solution)/shard_map/all_to_all | solution.py:95
  139.4 5.0 %collective-permute-start.6 = (f32[32768]{0:T(1024)S(1)}, f32[32768]{0:T(1024)S(1)}, u32[]{:S(2)}, u32[]{:S(2)}) collective-permute-start(f32[32768]{0:T(1024)S(1)} %bitcast.70), channel_id=1, source_target_pairs={{0,16},{1,17},{2,18},{3,19},{4,20},{5,21},{6,22},{7,23},{8,24},{9,... | collective-permute-start | bytes 393224 | tf_op jit(solution)/shard_map/ppermute | solution.py:35
  144.5 1.3 collective-permute-start.7
  145.8 10.4 %collective-permute-start.8 = (f32[8192]{0:T(1024)S(1)}, f32[8192]{0:T(1024)S(1)}, u32[]{:S(2)}, u32[]{:S(2)}) collective-permute-start(f32[8192]{0:T(1024)S(1)} %slice_select_fusion.1), channel_id=1, source_target_pairs={{0,4},{1,5},{2,6},{3,7},{4,0},{5,1},{6,2},{7,3},{8,12},{9,13},{10,... | collective-permute-start | bytes 98312 | tf_op jit(solution)/shard_map/ppermute | solution.py:35
  156.3 3.8 %collective-permute-start.9 = (f32[4096]{0:T(1024)S(1)}, f32[4096]{0:T(1024)S(1)}, u32[]{:S(2)}, u32[]{:S(2)}) collective-permute-start(f32[4096]{0:T(1024)S(1)} %slice_select_fusion.2), channel_id=1, source_target_pairs={{0,2},{1,3},{2,0},{3,1},{4,6},{5,7},{6,4},{7,5},{8,10},{9,11},{10,... | collective-permute-start | bytes 49160 | tf_op jit(solution)/shard_map/ppermute | solution.py:35
  160.1 3.7 %collective-permute-start.10 = (f32[2048]{0:T(1024)S(1)}, f32[2048]{0:T(1024)S(1)}, u32[]{:S(2)}, u32[]{:S(2)}) collective-permute-start(f32[2048]{0:T(1024)S(1)} %slice_select_fusion.3), channel_id=1, source_target_pairs={{0,1},{1,0},{2,3},{3,2},{4,5},{5,4},{6,7},{7,6},{8,9},{9,8},{10,11... | collective-permute-start | bytes 24584 | tf_op jit(solution)/shard_map/ppermute | solution.py:35
  163.8 3.7 %collective-permute-start.11 = (f32[2048]{0:T(1024)S(1)}, f32[2048]{0:T(1024)S(1)}, u32[]{:S(2)}, u32[]{:S(2)}) collective-permute-start(f32[2048]{0:T(1024)S(1)} %select_add_fusion.3), channel_id=1, source_target_pairs={{0,1},{1,0},{2,3},{3,2},{4,5},{5,4},{6,7},{7,6},{8,9},{9,8},{10,11... | collective-permute-start | bytes 24584 | tf_op jit(solution)/shard_map/ppermute | solution.py:35
  167.5 3.7 %collective-permute-start.12 = (f32[4096]{0:T(1024)S(1)}, f32[4096]{0:T(1024)S(1)}, u32[]{:S(2)}, u32[]{:S(2)}) collective-permute-start(f32[4096]{0:T(1024)S(1)} %maximum_select_fusion.6), channel_id=1, source_target_pairs={{0,2},{1,3},{2,0},{3,1},{4,6},{5,7},{6,4},{7,5},{8,10},{9,11},{10,... | collective-permute-start | bytes 49160 | tf_op jit(solution)/shard_map/ppermute | solution.py:35
  171.2 4.8 %collective-permute-start.13 = (f32[8192]{0:T(1024)S(1)}, f32[8192]{0:T(1024)S(1)}, u32[]{:S(2)}, u32[]{:S(2)}) collective-permute-start(f32[8192]{0:T(1024)S(1)} %maximum_select_fusion.5), channel_id=1, source_target_pairs={{0,4},{1,5},{2,6},{3,7},{4,0},{5,1},{6,2},{7,3},{8,12},{9,13},{10,... | collective-permute-start | bytes 98312 | tf_op jit(solution)/shard_map/ppermute | solution.py:35
  176.1 1.3 collective-permute-start.14
  177.4 5.6 %collective-permute-start.15 = (f32[32768]{0:T(1024)S(1)}, f32[32768]{0:T(1024)S(1)}, u32[]{:S(2)}, u32[]{:S(2)}) collective-permute-start(f32[32768]{0:T(1024)S(1)} %maximum_select_fusion.1), channel_id=1, source_target_pairs={{0,16},{1,17},{2,18},{3,19},{4,20},{5,21},{6,22},{7,23},{8,24},{9,... | collective-permute-start | bytes 393224 | tf_op jit(solution)/shard_map/ppermute | solution.py:35
where the time goes:
time: 249 us
  waiting for transfers between devices  104 us (42%)
  other arithmetic  71.6 us (29%)
  starting transfers between devices  38 us (15%)
  local copies, waits for them, and re-layouts  28.1 us (11%)
  matrix products  4.63 us (2%)
    ppermute x3, waiting for transfers between devices, with_halo(): lax.ppermute(tail, axis, [(i, (i + 1) % count) for i in range(ends)])  59.3 us
    another operation x7, other arithmetic, on_device(): factor = jnp.linalg.cholesky(gram)  34.9 us
    ppermute x10, waiting for transfers between devices, swapped(): return lax.ppermute(value, axis, pairs)  25.2 us
    all_to_all x1, waiting for transfers between devices, on_device(): lax.all_to_all(current, 'band', split_axis=2, concat_axis=0, tiled=True)  19.8 us
    another operation x4, other arithmetic, on_device(): lax.linalg.triangular_solve(factor, flat, left_side=True, lower=True)  19.8 us
    ppermute x10, starting transfers between devices, swapped(): return lax.ppermute(value, axis, pairs)  16.7 us
    ppermute x3, starting transfers between devices, with_halo(): lax.ppermute(tail, axis, [(i, (i + 1) % count) for i in range(ends)])  13.8 us
    unnamed x16, local copies, waits for them, and re-layouts  10.5 us
  transfers between devices with their start and end apart: 17, of which 14 were waited for; matrix products, arithmetic and copies ran while one was open for 1% of the time, Pallas kernels for 0%

commit v1 on v0

--- a/solution.py
+++ b/solution.py
@@ -92,7 +92,10 @@
         following = 2.0 * (applied - CENTRE * current) / HALF_WIDTH - earlier
         earlier = current
         current = following
-    regrouped = lax.all_to_all(current, "band", split_axis=2, concat_axis=0, tiled=True)
+    peers = lax.axis_size("band")
+    shards = jnp.stack(jnp.split(current, peers, axis=2), axis=0)
+    shards = lax.all_to_all(shards, "band", split_axis=0, concat_axis=0)
+    regrouped = jnp.concatenate(shards, axis=0)
     all_states = regrouped.shape[0]
     flat = regrouped.reshape(all_states, -1)
     cell_total = planes * plane_cells * lax.axis_size("space")

time: 249 us -> 231 us (0.928)
  local copies, waits for them, and re-layouts: 28.1 us -> 15.3 us
  other arithmetic: 71.6 us -> 67.7 us
    unnamed x16 -> x14, local copies, waits for them, and re-layouts: 10.5 us -> 1.82 us
    all_to_all x1 -> x0, other arithmetic: 5.21 us -> none  [on_device(): lax.all_to_all(current, 'band', split_axis=2, concat_axis=0, tiled=True)]
    all_to_all x2 -> x1, local copies, waits for them, and re-layouts: 3.82 us -> 0.95 us  [on_device(): shards = lax.all_to_all(shards, 'band', split_axis=0, concat_axis=0)]
    sub x1 -> x0, local copies, waits for them, and re-layouts: 2.72 us -> none  [on_device(): following = 2.0 * (applied - CENTRE * current) / HALF_WIDTH - earlier]
  transfers between devices with their start and end apart: 17 -> 17, of which waited for: 14 -> 14; matrix products, arithmetic and copies ran while one was open for 1% -> 2% of each run, Pallas kernels for 0% -> 0%
where the time goes in v1:
time: 231 us
  waiting for transfers between devices  103 us (45%)
  other arithmetic  67.7 us (29%)
  starting transfers between devices  38.2 us (17%)
  local copies, waits for them, and re-layouts  15.3 us (7%)
  matrix products  4.63 us (2%)
    ppermute x3, waiting for transfers between devices, with_halo(): lax.ppermute(tail, axis, [(i, (i + 1) % count) for i in range(ends)])  59.3 us
    another operation x7, other arithmetic, on_device(): factor = jnp.linalg.cholesky(gram)  34.9 us
    ppermute x10, waiting for transfers between devices, swapped(): return lax.ppermute(value, axis, pairs)  24.1 us
    all_to_all x1, waiting for transfers between devices, on_device(): shards = lax.all_to_all(shards, 'band', split_axis=0, concat_axis=0)  19.8 us
    another operation x4, other arithmetic, on_device(): lax.linalg.triangular_solve(factor, flat, left_side=True, lower=True)  19.8 us
    ppermute x10, starting transfers between devices, swapped(): return lax.ppermute(value, axis, pairs)  16.8 us
    ppermute x3, starting transfers between devices, with_halo(): lax.ppermute(tail, axis, [(i, (i + 1) % count) for i in range(ends)])  13.8 us
    sub x2, other arithmetic, on_device(): following = 2.0 * (applied - CENTRE * current) / HALF_WIDTH - earlier  7.6 us
  transfers between devices with their start and end apart: 17, of which 14 were waited for; matrix products, arithmetic and copies ran while one was open for 2% of the time, Pallas kernels for 0%

profile of v1, /device:TPU:0, one launch (start us, length us, event | category | flops | bytes accessed | tf_op | source)
XLA Modules:
  0.0 231.0 jit_solution(1369829151086823457)
XLA Ops:
  0.0 2.3 fusion.143
  2.3 5.0 %collective-permute-start = (f32[64,2,1024]{2,0,1:T(8,128)}, f32[64,2,1024]{2,0,1:T(8,128)S(1)}, u32[]{:S(2)}, u32[]{:S(2)}) collective-permute-start(f32[64,2,1024]{2,0,1:T(8,128)} %get-tuple-element.40), channel_id=1, source_target_pairs={{0,1},{1,2},{2,3},{3,4},{4,5},{5,6},{6,7},{8,9},{9,10},{10,11},{11... | collective-permute-start | bytes 1572872 | tf_op jit(solution)/shard_map/ppermute | solution.py:23
  7.3 1.3 collective-permute-start.1
  8.7 0.2 fusion.102
  8.9 0.2 reshape.99
  9.1 0.8 slice_reduce_fusion.2
  10.3 19.7 %collective-permute-done = f32[64,2,1024]{2,0,1:T(8,128)S(1)} collective-permute-done((f32[64,2,1024]{2,0,1:T(8,128)}, f32[64,2,1024]{2,0,1:T(8,128)S(1)}, u32[]{:S(2)}, u32[]{:S(2)}) %collective-permute-start) | collective-permute-done | bytes 524320 | tf_op jit(solution)/shard_map/ppermute | solution.py:23
  30.1 0.2 constant_dynamic-update-slice_fusion
  30.4 0.5 copy-done.2
  30.8 3.6 %broadcast_multiply_fusion = (f32[64,6,1024]{2,0,1:T(8,128)S(1)}, f32[64,6,1024]{2,0,1:T(8,128)S(1)}) fusion(f32[64,6,1024]{2,0,1:T(8,128)S(1)} %copy-done.1, f32[1024]{0:T(1024)S(1)} %get-tuple-element.52, f32[1024]{0:T(1024)S(1)} %get-tuple-element.53, f32[1024]{0:T(1024)S(1)} %fusion.136, f32[1024]{0:T(1024)S(1)} %get-tuple-element.54, ...), kind=kLoop, calls=%fused_computation.146 | loop fusion | flops 14548992 | bytes 11128832 | tf_op jit(solution)/shard_map/div | solution.py:89
  34.5 4.3 %collective-permute-start.2 = (f32[64,2,1024]{2,0,1:T(8,128)S(1)}, f32[64,2,1024]{2,0,1:T(8,128)S(1)}, u32[]{:S(2)}, u32[]{:S(2)}) collective-permute-start(f32[64,2,1024]{2,0,1:T(8,128)S(1)} %get-tuple-element.36), channel_id=1, source_target_pairs={{0,1},{1,2},{2,3},{3,4},{4,5},{5,6},{6,7},{8,9},{9,10},{10,11},{11... | collective-permute-start | bytes 1572872 | tf_op jit(solution)/shard_map/ppermute | solution.py:23
  38.8 1.3 collective-permute-start.3
  40.2 20.2 %collective-permute-done.2 = f32[64,2,1024]{2,0,1:T(8,128)S(1)} collective-permute-done((f32[64,2,1024]{2,0,1:T(8,128)S(1)}, f32[64,2,1024]{2,0,1:T(8,128)S(1)}, u32[]{:S(2)}, u32[]{:S(2)}) %collective-permute-start.2) | collective-permute-done | bytes 524320 | tf_op jit(solution)/shard_map/ppermute | solution.py:23
  60.3 3.8 %fusion.35 = f32[64,6,1024]{2,0,1:T(8,128)S(1)} fusion(f32[64,6,1024]{2,0,1:T(8,128)S(1)} %copy-done.1, f32[64,6,1024]{2,0,1:T(8,128)S(1)} %get-tuple-element.24, f32[64,2,1024]{2,0,1:T(8,128)S(1)} %collective-permute-done.3, f32[64,2,1024]{2,0,1:T(8,128)S(1)} %collective-permute-done.2, f32[64,6,1024]{2,0,1:T(8,128)S(1)} %get-tuple-element.25, ...), kind=kLoop, calls=%fused_computation.70 | loop fusion | flops 16515072 | bytes 7458816 | tf_op jit(solution)/shard_map/sub | solution.py:92
  64.3 4.4 %collective-permute-start.4 = (f32[64,2,1024]{2,0,1:T(8,128)S(1)}, f32[64,2,1024]{2,0,1:T(8,128)S(1)}, u32[]{:S(2)}, u32[]{:S(2)}) collective-permute-start(f32[64,2,1024]{2,0,1:T(8,128)S(1)} %get-tuple-element.34), channel_id=1, source_target_pairs={{0,1},{1,2},{2,3},{3,4},{4,5},{5,6},{6,7},{8,9},{9,10},{10,11},{11... | collective-permute-start | bytes 1572872 | tf_op jit(solution)/shard_map/ppermute | solution.py:23
  68.7 1.3 collective-permute-start.5
  70.0 19.4 %collective-permute-done.4 = f32[64,2,1024]{2,0,1:T(8,128)S(1)} collective-permute-done((f32[64,2,1024]{2,0,1:T(8,128)S(1)}, f32[64,2,1024]{2,0,1:T(8,128)S(1)}, u32[]{:S(2)}, u32[]{:S(2)}) %collective-permute-start.4) | collective-permute-done | bytes 524320 | tf_op jit(solution)/shard_map/ppermute | solution.py:23
  89.3 3.8 %fusion.60 = f32[64,6,1024]{2,0,1:T(8,128)S(1)} fusion(f32[64,6,1024]{2,0,1:T(8,128)S(1)} %fusion.35, f32[64,2,1024]{2,0,1:T(8,128)S(1)} %collective-permute-done.5, f32[64,2,1024]{2,0,1:T(8,128)S(1)} %collective-permute-done.4, f32[64,6,1024]{2,0,1:T(8,128)S(1)} %get-tuple-element.25, f32[1024]{0:T(1024)S(1)} %get-tuple-element.52, ...), kind=kLoop, calls=%fused_computation.95 | loop fusion | flops 16908288 | bytes 5885952 | tf_op jit(solution)/shard_map/sub | solution.py:92
  93.1 0.2 slice_bitcast_fusion.3
  93.3 1.3 pad_maximum_fusion.4
  94.6 3.7 %all-to-all-start = ((f32[4,64,6,256]{3,1,2,0:T(8,128)}), f32[4,64,6,256]{3,1,2,0:T(8,128)S(1)}, u32[]{:S(2)}, u32[]{:S(2)}) async-start(f32[4,64,6,256]{3,1,2,0:T(8,128)} %pad_maximum_fusion.4), calls=%async_computation | async-start | bytes 3145728 | tf_op jit(solution)/shard_map/all_to_all | solution.py:97
  98.4 19.8 %all-to-all-done = f32[4,64,6,256]{3,1,2,0:T(8,128)S(1)} async-done(((f32[4,64,6,256]{3,1,2,0:T(8,128)}), f32[4,64,6,256]{3,1,2,0:T(8,128)S(1)}, u32[]{:S(2)}, u32[]{:S(2)}) %all-to-all-start) | async-done | bytes 1572896 | tf_op jit(solution)/shard_map/all_to_all | solution.py:97
  118.2 0.9 copy.23
  119.2 0.7 copy.37
  119.8 1.4 fusion.144
  121.4 0.5 collective-permute-start.6
  121.9 4.5 %collective-permute-done.6 = f32[32768]{0:T(1024)S(1)} collective-permute-done((f32[32768]{0:T(1024)S(1)}, f32[32768]{0:T(1024)S(1)}, u32[]{:S(2)}, u32[]{:S(2)}) %collective-permute-start.6) | collective-permute-done | bytes 131104 | tf_op jit(solution)/shard_map/ppermute | solution.py:35
  126.6 1.2 collective-permute-done.7
  127.8 8.5 %collective-permute-start.8 = (f32[8192]{0:T(1024)S(1)}, f32[8192]{0:T(1024)S(1)}, u32[]{:S(2)}, u32[]{:S(2)}) collective-permute-start(f32[8192]{0:T(1024)S(1)} %slice_select_fusion.1), channel_id=1, source_target_pairs={{0,4},{1,5},{2,6},{3,7},{4,0},{5,1},{6,2},{7,3},{8,12},{9,13},{10,... | collective-permute-start | bytes 98312 | tf_op jit(solution)/shard_map/ppermute | solution.py:35
  136.4 1.9 collective-permute-done.8
  138.3 2.0 collective-permute-start.9
  140.2 1.8 collective-permute-done.9
  142.2 3.6 %collective-permute-done.10 = f32[2048]{0:T(1024)S(1)} collective-permute-done((f32[2048]{0:T(1024)S(1)}, f32[2048]{0:T(1024)S(1)}, u32[]{:S(2)}, u32[]{:S(2)}) %collective-permute-start.10) | collective-permute-done | bytes 8224 | tf_op jit(solution)/shard_map/ppermute | solution.py:35
  145.9 3.6 %collective-permute-done.11 = f32[2048]{0:T(1024)S(1)} collective-permute-done((f32[2048]{0:T(1024)S(1)}, f32[2048]{0:T(1024)S(1)}, u32[]{:S(2)}, u32[]{:S(2)}) %collective-permute-start.11) | collective-permute-done | bytes 8224 | tf_op jit(solution)/shard_map/ppermute | solution.py:35
  149.5 1.9 collective-permute-start.12
  151.4 0.1 fusion.140
  151.5 0.5 copy.33
  152.0 0.3 copy.40
  152.3 0.5 copy.34
  152.8 0.3 copy.41
  153.0 0.2 collective-permute-done.12
  153.2 2.9 %collective-permute-start.13 = (f32[8192]{0:T(1024)S(1)}, f32[8192]{0:T(1024)S(1)}, u32[]{:S(2)}, u32[]{:S(2)}) collective-permute-start(f32[8192]{0:T(1024)S(1)} %maximum_select_fusion.5), channel_id=1, source_target_pairs={{0,4},{1,5},{2,6},{3,7},{4,0},{5,1},{6,2},{7,3},{8,12},{9,13},{10,... | collective-permute-start | bytes 98312 | tf_op jit(solution)/shard_map/ppermute | solution.py:35
  156.3 1.7 collective-permute-done.13
  158.3 1.1 collective-permute-done.14
  159.4 0.8 collective-permute-start.15
  160.6 4.4 %collective-permute-done.15 = f32[32768]{0:T(1024)S(1)} collective-permute-done((f32[32768]{0:T(1024)S(1)}, f32[32768]{0:T(1024)S(1)}, u32[]{:S(2)}, u32[]{:S(2)}) %collective-permute-start.15) | collective-permute-done | bytes 131104 | tf_op jit(solution)/shard_map/ppermute | solution.py:35
  165.4 11.7 %cholesky.50 = f32[128,128]{1,0:T(8,128)S(1)} custom-call(f32[128,128]{1,0:T(8,128)S(1)} %cholesky.118), custom_call_target="Cholesky" | custom-call | tf_op jit(solution)/shard_map/jit(cholesky)/cholesky | solution.py:123
  177.1 10.0 %custom-call.14 = f32[1,128,128]{1,2,0:T(8,128)S(1)} custom-call(f32[1,128,128]{2,1,0:T(8,128)S(1)} %get-tuple-element.47), custom_call_target="InvertDiagBlocksLowerTriangular" | custom-call | tf_op jit(solution)/shard_map/jit(cholesky)/cholesky | solution.py:123
  187.1 0.2 constant_dynamic-update-slice_fusion.5
  187.3 0.3 convolution_subtract_fusion.1
  187.6 11.7 %cholesky.105 = f32[128,128]{1,0:T(8,128)S(1)} custom-call(f32[128,128]{1,0:T(8,128)S(1)} %convolution_subtract_fusion.1), custom_call_target="Cholesky" | custom-call | tf_op jit(solution)/shard_map/jit(cholesky)/cholesky | solution.py:123
  199.4 0.7 compare_reduce_fusion
  200.1 0.7 compare_reduce_fusion.1
  202.3 4.3 %while.1 = (s32[]{:T(128)}, f32[256,256]{1,0:T(8,128)S(1)}, s32[2,2]{1,0:T(2,128)S(1)}, f32[2,128,128]{2,1,0:T(8,128)S(1)}, s32[]{:T(128)}) while((s32[]{:T(128)}, f32[256,256]{1,0:T(8,128)S(1)}, s32[2,2]{1,0:T(2,128)S(1)}, f32[2,128,128]{2,1,0:T(8,128)S(1)}, s32[]{:T(128)}) %tuple.37), condition=%wide.while_cond, body=%wide.while_body.sunk | while | flops 2 | bytes 131181 | solution.py:124
  202.3 0.7 fusion.153
  203.0 1.5 bitcast_dynamic-update-slice_fusion.2
  204.5 0.7 fusion.153
  205.1 1.5 bitcast_dynamic-update-slice_fusion.2
  206.6 19.7 %custom-call.15 = f32[2,128,128]{1,2,0:T(8,128)S(1)} custom-call(f32[2,128,128]{2,1,0:T(8,128)S(1)} %get-tuple-element.12), custom_call_target="InvertDiagBlocksLowerTriangular" | custom-call | tf_op jit(solution)/shard_map/triangular_solve | solution.py:124
  226.3 0.8 fusion.105
  227.1 0.8 convolution_subtract_fusion
  227.9 0.8 fusion.104
  228.9 0.5 copy.35
  229.4 1.6 copy.36
  (70 shorter events, 2.5 us)
Async XLA Ops:
  0.0 8.6 %copy-start = (f32[64,96]{1,0:T(8,128)S(1)}, f32[64,96]{1,0:T(8,128)}, u32[]{:S(2)}) copy-start(f32[64,96]{1,0:T(8,128)} %param.6) | copy-start | bytes 73732
  0.0 8.6 %copy-start.3 = (s32[6,32]{1,0:T(8,128)S(1)}, s32[6,32]{1,0:T(8,128)}, u32[]{:S(2)}) copy-start(s32[6,32]{1,0:T(8,128)} %param.5) | copy-start | bytes 2308
  2.3 27.8 %copy-start.1 = (f32[64,6,1024]{2,0,1:T(8,128)S(1)}, f32[64,6,1024]{2,0,1:T(8,128)}, u32[]{:S(2)}) copy-start(f32[64,6,1024]{2,0,1:T(8,128)} %param.4) | copy-start | bytes 4718596
  2.3 27.7 %collective-permute-start = (f32[64,2,1024]{2,0,1:T(8,128)}, f32[64,2,1024]{2,0,1:T(8,128)S(1)}, u32[]{:S(2)}, u32[]{:S(2)}) collective-permute-start(f32[64,2,1024]{2,0,1:T(8,128)} %get-tuple-element.40), channel_id=1, source_target_pairs={{0,1},{1,2},{2,3},{3,4},{4,5},{5,6},{6,7},{8,9},{9,10},{10,11},{11... | collective-permute-start | bytes 1572872 | tf_op jit(solution)/shard_map/ppermute | solution.py:23
  7.3 23.0 %collective-permute-start.1 = (f32[64,2,1024]{2,0,1:T(8,128)}, f32[64,2,1024]{2,0,1:T(8,128)S(1)}, u32[]{:S(2)}, u32[]{:S(2)}) collective-permute-start(f32[64,2,1024]{2,0,1:T(8,128)} %get-tuple-element.41), channel_id=1, source_target_pairs={{1,0},{2,1},{3,2},{4,3},{5,4},{6,5},{7,6},{9,8},{10,9},{11,10},{12... | collective-permute-start | bytes 1572872 | tf_op jit(solution)/shard_map/ppermute | solution.py:25
  30.1 0.8 copy-start.2
  34.5 25.8 %collective-permute-start.2 = (f32[64,2,1024]{2,0,1:T(8,128)S(1)}, f32[64,2,1024]{2,0,1:T(8,128)S(1)}, u32[]{:S(2)}, u32[]{:S(2)}) collective-permute-start(f32[64,2,1024]{2,0,1:T(8,128)S(1)} %get-tuple-element.36), channel_id=1, source_target_pairs={{0,1},{1,2},{2,3},{3,4},{4,5},{5,6},{6,7},{8,9},{9,10},{10,11},{11... | collective-permute-start | bytes 1572872 | tf_op jit(solution)/shard_map/ppermute | solution.py:23
  38.8 21.5 %collective-permute-start.3 = (f32[64,2,1024]{2,0,1:T(8,128)S(1)}, f32[64,2,1024]{2,0,1:T(8,128)S(1)}, u32[]{:S(2)}, u32[]{:S(2)}) collective-permute-start(f32[64,2,1024]{2,0,1:T(8,128)S(1)} %get-tuple-element.37), channel_id=1, source_target_pairs={{1,0},{2,1},{3,2},{4,3},{5,4},{6,5},{7,6},{9,8},{10,9},{11,10},{12... | collective-permute-start | bytes 1572872 | tf_op jit(solution)/shard_map/ppermute | solution.py:25
  64.3 25.1 %collective-permute-start.4 = (f32[64,2,1024]{2,0,1:T(8,128)S(1)}, f32[64,2,1024]{2,0,1:T(8,128)S(1)}, u32[]{:S(2)}, u32[]{:S(2)}) collective-permute-start(f32[64,2,1024]{2,0,1:T(8,128)S(1)} %get-tuple-element.34), channel_id=1, source_target_pairs={{0,1},{1,2},{2,3},{3,4},{4,5},{5,6},{6,7},{8,9},{9,10},{10,11},{11... | collective-permute-start | bytes 1572872 | tf_op jit(solution)/shard_map/ppermute | solution.py:23
  68.7 20.7 %collective-permute-start.5 = (f32[64,2,1024]{2,0,1:T(8,128)S(1)}, f32[64,2,1024]{2,0,1:T(8,128)S(1)}, u32[]{:S(2)}, u32[]{:S(2)}) collective-permute-start(f32[64,2,1024]{2,0,1:T(8,128)S(1)} %get-tuple-element.35), channel_id=1, source_target_pairs={{1,0},{2,1},{3,2},{4,3},{5,4},{6,5},{7,6},{9,8},{10,9},{11,10},{12... | collective-permute-start | bytes 1572872 | tf_op jit(solution)/shard_map/ppermute | solution.py:25
  94.6 23.6 %all-to-all-start = ((f32[4,64,6,256]{3,1,2,0:T(8,128)}), f32[4,64,6,256]{3,1,2,0:T(8,128)S(1)}, u32[]{:S(2)}, u32[]{:S(2)}) async-start(f32[4,64,6,256]{3,1,2,0:T(8,128)} %pad_maximum_fusion.4), calls=%async_computation | async-start | bytes 3145728 | tf_op jit(solution)/shard_map/all_to_all | solution.py:97
  121.4 5.0 %collective-permute-start.6 = (f32[32768]{0:T(1024)S(1)}, f32[32768]{0:T(1024)S(1)}, u32[]{:S(2)}, u32[]{:S(2)}) collective-permute-start(f32[32768]{0:T(1024)S(1)} %bitcast.71), channel_id=1, source_target_pairs={{0,16},{1,17},{2,18},{3,19},{4,20},{5,21},{6,22},{7,23},{8,24},{9,... | collective-permute-start | bytes 393224 | tf_op jit(solution)/shard_map/ppermute | solution.py:35
  126.5 1.3 collective-permute-start.7
  127.8 10.4 %collective-permute-start.8 = (f32[8192]{0:T(1024)S(1)}, f32[8192]{0:T(1024)S(1)}, u32[]{:S(2)}, u32[]{:S(2)}) collective-permute-start(f32[8192]{0:T(1024)S(1)} %slice_select_fusion.1), channel_id=1, source_target_pairs={{0,4},{1,5},{2,6},{3,7},{4,0},{5,1},{6,2},{7,3},{8,12},{9,13},{10,... | collective-permute-start | bytes 98312 | tf_op jit(solution)/shard_map/ppermute | solution.py:35
  138.3 3.8 %collective-permute-start.9 = (f32[4096]{0:T(1024)S(1)}, f32[4096]{0:T(1024)S(1)}, u32[]{:S(2)}, u32[]{:S(2)}) collective-permute-start(f32[4096]{0:T(1024)S(1)} %slice_select_fusion.2), channel_id=1, source_target_pairs={{0,2},{1,3},{2,0},{3,1},{4,6},{5,7},{6,4},{7,5},{8,10},{9,11},{10,... | collective-permute-start | bytes 49160 | tf_op jit(solution)/shard_map/ppermute | solution.py:35
  142.1 3.7 %collective-permute-start.10 = (f32[2048]{0:T(1024)S(1)}, f32[2048]{0:T(1024)S(1)}, u32[]{:S(2)}, u32[]{:S(2)}) collective-permute-start(f32[2048]{0:T(1024)S(1)} %slice_select_fusion.3), channel_id=1, source_target_pairs={{0,1},{1,0},{2,3},{3,2},{4,5},{5,4},{6,7},{7,6},{8,9},{9,8},{10,11... | collective-permute-start | bytes 24584 | tf_op jit(solution)/shard_map/ppermute | solution.py:35
  145.8 3.7 %collective-permute-start.11 = (f32[2048]{0:T(1024)S(1)}, f32[2048]{0:T(1024)S(1)}, u32[]{:S(2)}, u32[]{:S(2)}) collective-permute-start(f32[2048]{0:T(1024)S(1)} %select_add_fusion.3), channel_id=1, source_target_pairs={{0,1},{1,0},{2,3},{3,2},{4,5},{5,4},{6,7},{7,6},{8,9},{9,8},{10,11... | collective-permute-start | bytes 24584 | tf_op jit(solution)/shard_map/ppermute | solution.py:35
  149.5 3.7 %collective-permute-start.12 = (f32[4096]{0:T(1024)S(1)}, f32[4096]{0:T(1024)S(1)}, u32[]{:S(2)}, u32[]{:S(2)}) collective-permute-start(f32[4096]{0:T(1024)S(1)} %maximum_select_fusion.6), channel_id=1, source_target_pairs={{0,2},{1,3},{2,0},{3,1},{4,6},{5,7},{6,4},{7,5},{8,10},{9,11},{10,... | collective-permute-start | bytes 49160 | tf_op jit(solution)/shard_map/ppermute | solution.py:35
  153.2 4.8 %collective-permute-start.13 = (f32[8192]{0:T(1024)S(1)}, f32[8192]{0:T(1024)S(1)}, u32[]{:S(2)}, u32[]{:S(2)}) collective-permute-start(f32[8192]{0:T(1024)S(1)} %maximum_select_fusion.5), channel_id=1, source_target_pairs={{0,4},{1,5},{2,6},{3,7},{4,0},{5,1},{6,2},{7,3},{8,12},{9,13},{10,... | collective-permute-start | bytes 98312 | tf_op jit(solution)/shard_map/ppermute | solution.py:35
  158.0 1.3 collective-permute-start.14
  159.4 5.6 %collective-permute-start.15 = (f32[32768]{0:T(1024)S(1)}, f32[32768]{0:T(1024)S(1)}, u32[]{:S(2)}, u32[]{:S(2)}) collective-permute-start(f32[32768]{0:T(1024)S(1)} %maximum_select_fusion.1), channel_id=1, source_target_pairs={{0,16},{1,17},{2,18},{3,19},{4,20},{5,21},{6,22},{7,23},{8,24},{9,... | collective-permute-start | bytes 393224 | tf_op jit(solution)/shard_map/ppermute | solution.py:35
